TPU v7x, 32 devices: a whole 2x2x4 slice. The times are simulated.
32 devices in a mesh: slab: 4 (over y, x), leaf: 8 (over z, core).
Axes of the slice: x: 2, y: 2, z: 4, core: 2. Of those that a mesh axis runs over, the one named last changes fastest.
Arguments:
- right_sides: bfloat16 [32, 131072], P(None, ('slab', 'leaf')), may hold values from -6 to 6
- left_sides: bfloat16 [32, 131072], P(None, ('slab', 'leaf')), may hold values from -6 to 6
- near_blocks: bfloat16 [1024, 8, 128, 128], P(('slab', 'leaf')), may hold values from -0.1875 to 0.1875
- near_columns: int32 [1024, 8], P(('slab', 'leaf')), may hold values from 0 to 1023, as said below
- cluster_points: int32 [1024], P(('slab', 'leaf')), may hold values from 64 to 128, as said below
- leaf_basis: bfloat16 [1024, 64, 128], P(('slab', 'leaf')), may hold values from -0.5 to 0.5
- transfer: float32 [1024, 64, 128], P(('slab', 'leaf')), may hold values from -0.625 to 0.625
- far_parents: int32 [32, 24], P(('slab', 'leaf')), may hold values from 0 to 31, as said below
- far_count: int32 [32], P(('slab', 'leaf')), may hold values from 12 to 24, as said below
- coupling: float32 [32, 24, 128, 128], P(('slab', 'leaf')), may hold values from -0.375 to 0.375
- slab_transfer: float32 [32, 128, 128], P(('slab', 'leaf')), may hold values from -0.75 to 0.75
- apex_coupling: float32 [4, 4, 128, 128], replicated, may hold values from -0.75 to 0.75
Outputs:
- product: float32 [32, 131072], P(None, ('slab', 'leaf'))
- adjoint_product: float32 [32, 131072], P(None, ('slab', 'leaf'))
Inputs may be any that keep to these rules, and one draw needn't show every extreme that they name: `near_columns`: row i holds 8 different clusters, i among them, all inside the window of 9 consecutive clusters centred on i, moved inward where it would pass an end of 0 to 1023. `cluster_points`: some cluster has exactly 128 points and some exactly 64. `far_parents`: row p holds 24 different parents, none equal to p; only the first far_count[p] are used. `far_count`: some parent uses all 24 slots and some exactly 12.
All inputs are finite; a program needn't handle non-finite values.
Results may differ from a plain program's by a relative error of at most 0.0024.
Values may be sent and summed in bfloat16 or wider, within the bound.
A program may use at most 128 MiB of HBM per device.

v0:
```python
import functools

import jax
import jax.numpy as jnp
from jax import lax
from jax.experimental import pallas as pl
from jax.experimental.pallas import tpu as pltpu
from jax.sharding import PartitionSpec as P

B = 128
HW = 4
BF = jnp.bfloat16
F32 = jnp.float32
MESH = pl.DeviceIdType.MESH


def nt(a, b):
    return lax.dot_general(a, b, (((1,), (1,)), ((), ())), preferred_element_type=F32)


def nn(a, b):
    return lax.dot_general(a, b, (((1,), (0,)), ((), ())), preferred_element_type=F32)


def split(x):
    high = x.astype(BF)
    return high, (x - high.astype(F32)).astype(BF)


def three(a, b, product):
    rows = a.shape[0]
    ah, al = split(a)
    bh, bl = split(b)
    both = product(jnp.concatenate([ah, al], axis=0), bh)
    return both[:rows] + both[rows:] + product(ah, bl)


def kernel(
    slabs,
    leaves,
    points_s,
    targets_s,
    count_s,
    columns_h,
    right_h,
    left_h,
    basis_h,
    transfer_h,
    lift_h,
    coupling_h,
    apex_h,
    near_h,
    hat_ref,
    near_h_out,
    back_h_out,
    right_v,
    left_v,
    basis_v,
    transfer_v,
    lift_v,
    coupling_v,
    apex_row_v,
    apex_col_v,
    near_v,
    columns_v,
    table_v,
    far_table_v,
    table_s,
    far_table_s,
    ext_v,
    masked_left_v,
    collected_v,
    near_out_v,
    edge_out_v,
    edge_in_v,
    share_v,
    share_in_v,
    slab_v,
    parents_v,
    outward_v,
    arrived_v,
    in_sem,
    table_sem,
    halo_send,
    halo_recv,
    edge_send,
    edge_recv,
    share_send,
    share_recv,
    slab_send,
    slab_recv,
    parent_send,
    parent_recv,
    out_send,
    out_recv,
):
    rhs = right_h.shape[0]
    slots, clusters = columns_v.shape
    rank = basis_v.shape[1]
    far_slots = coupling_v.shape[0]
    devices = slabs * leaves
    width = 2 * HW + 1
    my_slab = lax.axis_index("slab")
    my_leaf = lax.axis_index("leaf")
    me = my_slab * leaves + my_leaf
    first = 1 - (me + devices - 1) // devices
    last = (me + 1) // devices

    def place(d):
        return (d // leaves, d % leaves)

    ext_v[0:HW] = jnp.zeros((HW, rhs, B), BF)
    ext_v[clusters + HW :] = jnp.zeros((HW, rhs, B), BF)
    edge_in_v[...] = jnp.zeros_like(edge_in_v)

    inputs = [
        pltpu.make_async_copy(src, dst, in_sem.at[i])
        for i, (src, dst) in enumerate(
            [
                (right_h, right_v),
                (left_h, left_v),
                (basis_h, basis_v),
                (transfer_h, transfer_v),
                (lift_h, lift_v),
                (coupling_h, coupling_v),
                (near_h, near_v.at[pl.ds(0, clusters * slots)]),
                (apex_h.at[my_slab], apex_row_v),
                (apex_h.at[:, my_slab], apex_col_v),
                (columns_h, columns_v),
            ]
        )
    ]
    inputs[9].start()
    for copy in inputs[:9]:
        copy.start()

    barrier = pltpu.get_barrier_semaphore()

    def greet(k, _):
        pl.semaphore_signal(
            barrier, inc=1, device_id=place((me + k) % devices), device_id_type=MESH
        )
        return 0

    lax.fori_loop(1, devices, greet, 0)

    collected_v[...] = jnp.zeros_like(collected_v)
    near_v[clusters * slots] = jnp.zeros((B, B), BF)

    inputs[9].wait()
    row = lax.broadcasted_iota(jnp.int32, (1, clusters), 1)
    opening = (
        row
        + first * jnp.maximum(HW - row, 0)
        - last * jnp.maximum(row - (clusters - HW - 1), 0)
    )
    spots = [columns_v[s : s + 1] - (me * clusters - HW) for s in range(slots)]
    for w in range(width):
        found = jnp.full((1, clusters), clusters * slots, jnp.int32)
        for s in range(slots):
            found = jnp.where(spots[s] == opening + w, row * slots + s, found)
        table_v[w : w + 1] = found
    for s in range(slots):
        table_v[width + s : width + s + 1] = jnp.clip(spots[s], 0, clusters + 2 * HW - 1)
    owner = lax.broadcasted_iota(jnp.int32, (1, devices), 1)
    found = jnp.full((1, devices), -1, jnp.int32)
    for f in range(far_slots):
        target = jnp.where(f < count_s[0], targets_s[f], -1)
        found = jnp.where(owner == target, f, found)
    far_table_v[0:1] = found
    tables = [
        pltpu.make_async_copy(table_v, table_s, table_sem.at[0]),
        pltpu.make_async_copy(far_table_v, far_table_s, table_sem.at[1]),
    ]
    for copy in tables:
        copy.start()

    for copy in inputs[:4]:
        copy.wait()

    lane = lax.broadcasted_iota(jnp.int32, (rhs, B), 1)

    def window(c):
        return pl.ds(pl.multiple_of(c * B, B), B)

    def mask_of(c):
        return jnp.where(lane < points_s[c], 1.0, 0.0)

    def leaf_step(c, total):
        mask = mask_of(c).astype(BF)
        r = right_v[:, window(c)] * mask
        l = left_v[:, window(c)] * mask
        ext_v[c + HW] = r
        masked_left_v[c] = l
        leaf = nt(jnp.concatenate([r, l], axis=0), basis_v[c])
        return total + three(leaf, transfer_v[c], nn)

    unroll = 4

    def leaf_group(g, total):
        for u in range(unroll):
            total = leaf_step(g * unroll + u, total)
        return total

    parent = lax.fori_loop(
        0, clusters // unroll, leaf_group, jnp.zeros((2 * rhs, transfer_v.shape[2]), F32)
    )

    parents_v[me] = parent[:rhs].astype(BF)
    inputs[4].wait()
    share = three(parent, lift_v[...], nn)
    chunk = share_v.shape[1]
    for j in range(leaves):
        share_v[j] = share[j * chunk : (j + 1) * chunk]

    pl.semaphore_wait(barrier, devices - 1)

    def halo_copy(to_next):
        where = me + 1 if to_next else me - 1
        src = clusters if to_next else HW
        dst = 0 if to_next else clusters + HW
        i = 0 if to_next else 1
        return pltpu.make_async_remote_copy(
            src_ref=ext_v.at[pl.ds(src, HW)],
            dst_ref=ext_v.at[pl.ds(dst, HW)],
            send_sem=halo_send.at[i],
            recv_sem=halo_recv.at[i],
            device_id=place(where),
            device_id_type=MESH,
        )

    def share_copy(k):
        peer = (my_leaf + k) % leaves
        return pltpu.make_async_remote_copy(
            src_ref=share_v.at[peer],
            dst_ref=share_in_v.at[my_leaf],
            send_sem=share_send.at[k],
            recv_sem=share_recv.at[k],
            device_id=(my_slab, peer),
            device_id_type=MESH,
        )

    def share_arrival(k):
        peer = (my_leaf + leaves - k) % leaves
        return pltpu.make_async_remote_copy(
            src_ref=share_v.at[my_leaf],
            dst_ref=share_in_v.at[peer],
            send_sem=share_send.at[k],
            recv_sem=share_recv.at[k],
            device_id=(my_slab, peer),
            device_id_type=MESH,
        )

    def wide_copy(k, src, dst, send, recv, spread):
        peer = (me + k) % devices
        return pltpu.make_async_remote_copy(
            src_ref=src.at[peer if spread else me],
            dst_ref=dst.at[me],
            send_sem=send.at[k],
            recv_sem=recv.at[k],
            device_id=place(peer),
            device_id_type=MESH,
        )

    def wide_arrival(k, src, dst, send, recv):
        peer = (me + devices - k) % devices
        return pltpu.make_async_remote_copy(
            src_ref=src.at[me],
            dst_ref=dst.at[peer],
            send_sem=send.at[k],
            recv_sem=recv.at[k],
            device_id=place(peer),
            device_id_type=MESH,
        )

    def loop(low, high, act):
        def step(k, carry):
            act(k)
            return carry

        lax.fori_loop(low, high, step, 0)

    loop(1, leaves, lambda k: share_copy(k).start())
    share_in_v[my_leaf] = share_v[my_leaf]

    @pl.when(me < devices - 1)
    def _():
        halo_copy(True).start()

    @pl.when(me > 0)
    def _():
        halo_copy(False).start()

    loop(
        1,
        devices,
        lambda k: wide_copy(k, parents_v, parents_v, parent_send, parent_recv, False).start(),
    )

    inputs[5].wait()
    for copy in tables:
        copy.wait()
    lh, ll = split(parent[rhs:])
    left_both = jnp.concatenate([lh, ll], axis=0)

    def outward(q):
        f = far_table_s[0, q]
        live = jnp.where(f >= 0, 1.0, 0.0)
        ch, cl = split(coupling_v[jnp.maximum(f, 0)])
        both = nn(left_both, ch)
        term = both[:rhs] + both[rhs:] + nn(lh, cl)
        outward_v[q] = (term * live).astype(BF)

    def outward_group(g):
        for u in range(unroll):
            outward(g * unroll + u)

    loop(0, devices // unroll, outward_group)
    arrived_v[me] = jnp.zeros((rhs, arrived_v.shape[2]), BF)

    loop(1, leaves, lambda k: share_arrival(k).wait_recv())
    total = share_in_v[0]
    for j in range(1, leaves):
        total = total + share_in_v[j]
    slab_v[me] = total

    loop(1, devices, lambda k: wide_copy(k, slab_v, slab_v, slab_send, slab_recv, False).start())
    loop(
        1,
        devices,
        lambda k: wide_copy(k, outward_v, arrived_v, out_send, out_recv, True).start(),
    )

    inputs[6].wait()

    def near_back(i, e0):
        left = masked_left_v[i]
        for w in range(width):
            collected_v[e0 + w] += nn(left, near_v[table_s[w, i]])

    def near_forward(i):
        blocks = jnp.concatenate([near_v[i * slots + s] for s in range(slots)], axis=1)
        picked = jnp.concatenate([ext_v[table_s[width + s, i]] for s in range(slots)], axis=1)
        near_out_v[i] = nt(picked, blocks)

    for i in range(HW):
        near_back(i, i + first * (HW - i))
    for i in range(clusters - HW, clusters):
        near_back(i, i - last * (i - (clusters - HW - 1)))

    edge_out_v[0] = collected_v[0:HW].astype(BF)
    edge_out_v[1] = collected_v[clusters + HW :].astype(BF)

    def edge_copy(to_next):
        i = 1 if to_next else 0
        return pltpu.make_async_remote_copy(
            src_ref=edge_out_v.at[i],
            dst_ref=edge_in_v.at[i],
            send_sem=edge_send.at[i],
            recv_sem=edge_recv.at[i],
            device_id=place(me + 1 if to_next else me - 1),
            device_id_type=MESH,
        )

    @pl.when(me < devices - 1)
    def _():
        edge_copy(True).start()

    @pl.when(me > 0)
    def _():
        edge_copy(False).start()

    @pl.when(me > 0)
    def _():
        halo_copy(True).wait_recv()

    @pl.when(me < devices - 1)
    def _():
        halo_copy(False).wait_recv()

    for i in list(range(HW)) + list(range(clusters - HW, clusters)):
        near_forward(i)

    def middle(g):
        i = HW + g * HW
        lefts = [masked_left_v[i + u] for u in range(HW)]
        for e in range(width + HW - 1):
            rows = [u for u in range(HW) if 0 <= e - u < width]
            left = jnp.concatenate([lefts[u] for u in rows], axis=1)
            blocks = jnp.concatenate([near_v[table_s[e - u, i + u]] for u in rows], axis=0)
            collected_v[i + e] += nn(left, blocks)
        for u in range(HW):
            near_forward(i + u)

    loop(0, (clusters - 2 * HW) // HW, middle)

    @pl.when(me > 0)
    def _():
        edge_copy(True).wait_recv()

    @pl.when(me < devices - 1)
    def _():
        edge_copy(False).wait_recv()

    collected_v[HW : 2 * HW] += edge_in_v[1].astype(F32)
    collected_v[clusters : clusters + HW] += edge_in_v[0].astype(F32)

    results = [
        pltpu.make_async_copy(near_out_v, near_h_out, table_sem.at[0]),
        pltpu.make_async_copy(
            collected_v.at[pl.ds(HW, clusters)], back_h_out, table_sem.at[1]
        ),
    ]
    for copy in results:
        copy.start()

    loop(1, devices, lambda k: wide_arrival(k, slab_v, slab_v, slab_send, slab_recv).wait_recv())
    inputs[7].wait()
    inputs[8].wait()
    apex_right = jnp.zeros((rhs, lift_v.shape[1]), F32)
    apex_left = jnp.zeros((rhs, lift_v.shape[1]), F32)
    for t in range(slabs):
        other = jnp.where(my_slab == t, 0.0, 1.0)
        whole = jnp.concatenate([slab_v[t * leaves + j] for j in range(leaves)], axis=0)
        apex_right += other * three(whole[:rhs], apex_row_v[t], nt)
        apex_left += other * three(whole[rhs:], apex_col_v[t], nn)
    spread = three(jnp.concatenate([apex_right, apex_left], axis=0), lift_v[...], nt)

    loop(
        1,
        devices,
        lambda k: wide_arrival(k, parents_v, parents_v, parent_send, parent_recv).wait_recv(),
    )

    def far(f, total):
        live = jnp.where(f < count_s[0], 1.0, 0.0)
        ch, cl = split(coupling_v[f])
        chosen = parents_v[targets_s[f]]
        return total + live * (nt(chosen, ch) + nt(chosen, cl))

    def far_group(g, total):
        for u in range(unroll):
            total = far(g * unroll + u, total)
        return total

    far_right = lax.fori_loop(0, far_slots // unroll, far_group, spread[:rhs])

    loop(
        1, devices, lambda k: wide_arrival(k, outward_v, arrived_v, out_send, out_recv).wait_recv()
    )
    far_left = lax.fori_loop(
        0, devices, lambda d, total: total + arrived_v[d].astype(F32), spread[rhs:]
    )

    hat_ref[:rhs] = far_right
    hat_ref[rhs:] = far_left
    for copy in results:
        copy.wait()

    loop(1, leaves, lambda k: share_copy(k).wait_send())
    loop(1, devices, lambda k: wide_copy(k, slab_v, slab_v, slab_send, slab_recv, False).wait_send())
    loop(
        1,
        devices,
        lambda k: wide_copy(k, parents_v, parents_v, parent_send, parent_recv, False).wait_send(),
    )
    loop(
        1,
        devices,
        lambda k: wide_copy(k, outward_v, arrived_v, out_send, out_recv, True).wait_send(),
    )

    @pl.when(me < devices - 1)
    def _():
        halo_copy(True).wait_send()
        edge_copy(True).wait_send()

    @pl.when(me > 0)
    def _():
        halo_copy(False).wait_send()
        edge_copy(False).wait_send()


def finish_kernel(
    points_s, hat_ref, transfer_ref, basis_ref, near_ref, back_ref, product_ref, adjoint_ref
):
    group = transfer_ref.shape[0]
    rhs = near_ref.shape[1]
    hh, hl = split(hat_ref[...])
    hat_both = jnp.concatenate([hh, hl], axis=0)
    lane = lax.broadcasted_iota(jnp.int32, (rhs, B), 1)
    for c in range(group):
        th, tl = split(transfer_ref[c])
        both = nt(hat_both, th)
        down = (both[: 2 * rhs] + both[2 * rhs :] + nt(hh, tl)).astype(BF)
        out = nn(down, basis_ref[c])
        keep = lane < points_s[pl.program_id(0) * group + c]
        columns = slice(c * B, (c + 1) * B)
        product_ref[:, columns] = jnp.where(keep, near_ref[c] + out[:rhs], 0.0)
        adjoint_ref[:, columns] = jnp.where(keep, back_ref[c] + out[rhs:], 0.0)


def shards(
    right_sides,
    left_sides,
    near_blocks,
    near_columns,
    cluster_points,
    leaf_basis,
    transfer,
    far_parents,
    far_count,
    coupling,
    slab_transfer,
    apex_coupling,
):
    slabs, leaves = lax.axis_size("slab"), lax.axis_size("leaf")
    devices = slabs * leaves
    rhs, columns = right_sides.shape
    clusters, slots = near_columns.shape
    rank, k2 = transfer.shape[1:]
    k3 = slab_transfer.shape[2]
    width = 2 * HW + 1
    chunk = 2 * rhs // leaves
    smem = pl.BlockSpec(memory_space=pltpu.SMEM)
    hbm = pl.BlockSpec(memory_space=pltpu.HBM)
    vmem = pl.BlockSpec(memory_space=pltpu.VMEM)
    dma = pltpu.SemaphoreType.DMA
    out = jax.ShapeDtypeStruct((rhs, columns), F32)
    blocks = jax.ShapeDtypeStruct((clusters, rhs, B), F32)
    hat, near_out, near_back = pl.pallas_call(
        functools.partial(kernel, slabs, leaves),
        out_shape=(jax.ShapeDtypeStruct((2 * rhs, k2), F32), blocks, blocks),
        in_specs=[smem] * 3 + [hbm] * 9,
        out_specs=(vmem, hbm, hbm),
        scratch_shapes=[
            pltpu.VMEM((rhs, columns), BF),
            pltpu.VMEM((rhs, columns), BF),
            pltpu.VMEM(leaf_basis.shape, BF),
            pltpu.VMEM(transfer.shape, F32),
            pltpu.VMEM((k2, k3), F32),
            pltpu.VMEM(coupling.shape[1:], F32),
            pltpu.VMEM((slabs, k3, k3), F32),
            pltpu.VMEM((slabs, k3, k3), F32),
            pltpu.VMEM((clusters * slots + 1, B, B), BF),
            pltpu.VMEM((slots, clusters), jnp.int32),
            pltpu.VMEM((width + slots, clusters), jnp.int32),
            pltpu.VMEM((1, devices), jnp.int32),
            pltpu.SMEM((width + slots, clusters), jnp.int32),
            pltpu.SMEM((1, devices), jnp.int32),
            pltpu.VMEM((clusters + 2 * HW, rhs, B), BF),
            pltpu.VMEM((clusters, rhs, B), BF),
            pltpu.VMEM((clusters + 2 * HW, rhs, B), F32),
            pltpu.VMEM((clusters, rhs, B), F32),
            pltpu.VMEM((2, HW, rhs, B), BF),
            pltpu.VMEM((2, HW, rhs, B), BF),
            pltpu.VMEM((leaves, chunk, k3), F32),
            pltpu.VMEM((leaves, chunk, k3), F32),
            pltpu.VMEM((devices, chunk, k3), F32),
            pltpu.VMEM((devices, rhs, k2), BF),
            pltpu.VMEM((devices, rhs, k2), BF),
            pltpu.VMEM((devices, rhs, k2), BF),
            dma((10,)),
            dma((2,)),
            dma((2,)),
            dma((2,)),
            dma((2,)),
            dma((2,)),
            dma((leaves,)),
            dma((leaves,)),
            dma((devices,)),
            dma((devices,)),
            dma((devices,)),
            dma((devices,)),
            dma((devices,)),
            dma((devices,)),
        ],
        compiler_params=pltpu.CompilerParams(
            collective_id=0, has_side_effects=True, vmem_limit_bytes=60 * 1024 * 1024
        ),
        name="h2_step",
    )(
        cluster_points,
        far_parents[0],
        far_count,
        near_columns.T,
        right_sides,
        left_sides,
        leaf_basis,
        transfer,
        slab_transfer[0],
        coupling[0],
        apex_coupling,
        near_blocks.reshape(-1, B, B),
    )
    group = 8
    return pl.pallas_call(
        finish_kernel,
        out_shape=(out, out),
        grid=(clusters // group,),
        in_specs=[
            smem,
            pl.BlockSpec((2 * rhs, k2), lambda g: (0, 0)),
            pl.BlockSpec((group, rank, k2), lambda g: (g, 0, 0)),
            pl.BlockSpec((group, rank, B), lambda g: (g, 0, 0)),
            pl.BlockSpec((group, rhs, B), lambda g: (g, 0, 0)),
            pl.BlockSpec((group, rhs, B), lambda g: (g, 0, 0)),
        ],
        out_specs=(
            pl.BlockSpec((rhs, group * B), lambda g: (0, g)),
            pl.BlockSpec((rhs, group * B), lambda g: (0, g)),
        ),
        name="h2_finish",
    )(cluster_points, hat, transfer, leaf_basis, near_out, near_back)


def solution(mesh):
    return jax.shard_map(
        shards,
        mesh=mesh,
        in_specs=(
            P(None, ("slab", "leaf")),
            P(None, ("slab", "leaf")),
            P(("slab", "leaf"), None, None, None),
            P(("slab", "leaf"), None),
            P(("slab", "leaf")),
            P(("slab", "leaf"), None, None),
            P(("slab", "leaf"), None, None),
            P(("slab", "leaf"), None),
            P(("slab", "leaf")),
            P(("slab", "leaf"), None, None, None),
            P(("slab", "leaf"), None, None),
            P(),
        ),
        out_specs=(P(None, ("slab", "leaf")), P(None, ("slab", "leaf"))),
        check_vma=False,
    )
```

profile of v0, /device:TPU:0, one launch (start us, length us, event | category | flops | bytes accessed | tf_op | source)
XLA Modules:
  0.0 40.1 jit_solution(9584614121025513089)
XLA Ops:
  1.3 31.4 %h2_step.1 = (f32[64,128]{1,0:T(8,128)}, f32[32,32,128]{2,1,0:T(8,128)}, f32[32,32,128]{2,1,0:T(8,128)}) custom-call(s32[32]{0:T(128)} %points_s.3, s32[24]{0:T(128)} %bitcast.9, s32[1]{0:T(128)S(6)} %copy.14.count_s, s32[8,32]{1,0:T(8,128)} %bitcast.8, bf16[32,4096]{1,0:T(8,128)(2,1)} %right_h.1, bf16[32,4096]{1,0:T(8,128)(2,1)} %left_h.1, ...), custom_call_target="tpu_custom_call" | custom-call | tf_op jit(solution)/shard_map/h2_step/pallas_call | solution.py:531
  32.7 7.4 %h2_finish.1 = (f32[32,4096]{1,0:T(8,128)}, f32[32,4096]{1,0:T(8,128)}) custom-call(s32[32]{0:T(128)} %points_s.3, f32[64,128]{1,0:T(8,128)} %get-tuple-element.5.hat_ref, f32[32,64,128]{2,1,0:T(8,128)} %transfer_ref.1, bf16[32,64,128]{2,1,0:T(8,128)(2,1)} %basis_ref.1, f32[32,32,128]{2,1,0:T(8,128)} %get-tuple-element.6.near_ref, ...), custom_call_target="tpu_custom_call" | custom-call | tf_op jit(solution)/shard_map/h2_finish/pallas_call | solution.py:597
where the time goes:
time: 40.2 us; the launch traced here: 40.1 us
  Pallas kernels  38.8 us (97%)
  between operations  1.29 us (3%)
    pallas_call x1, Pallas kernels, shards(): pl.pallas_call(functools.partial(kernel, slabs, leaves), out_shape=(jax.S...  31.4 us
    pallas_call x1, Pallas kernels, shards(): pl.pallas_call(finish_kernel, out_shape=(out, out), grid=(clusters // gro...  7.35 us

commit v1 on v0

v1 whole, which is shorter than its diff:
```python
import functools

import jax
import jax.numpy as jnp
from jax import lax
from jax.experimental import pallas as pl
from jax.experimental.pallas import tpu as pltpu
from jax.sharding import PartitionSpec as P

B = 128
HW = 4
CORES = 2
BF = jnp.bfloat16
F32 = jnp.float32
MESH = pl.DeviceIdType.MESH


def nt(a, b):
    return lax.dot_general(a, b, (((1,), (1,)), ((), ())), preferred_element_type=F32)


def nn(a, b):
    return lax.dot_general(a, b, (((1,), (0,)), ((), ())), preferred_element_type=F32)


def split(x):
    high = x.astype(BF)
    return high, (x - high.astype(F32)).astype(BF)


def stacked(x):
    return jnp.concatenate(split(x), axis=0)


def wide(x):
    return jnp.concatenate(split(x), axis=1)


def three_nn(a, pair):
    rows, columns = a.shape[0], pair.shape[1] // 2
    both = nn(stacked(a), pair)
    return both[:rows, :columns] + both[rows:, :columns] + both[:rows, columns:]


def paired_rows(a):
    high, low = split(a)
    return jnp.concatenate(
        [
            jnp.concatenate([high, high], axis=1),
            jnp.concatenate([low, jnp.zeros_like(low)], axis=1),
        ],
        axis=0,
    )


def three_nt(a, pair):
    rows = a.shape[0]
    both = nt(paired_rows(a), pair)
    return both[:rows] + both[rows:]


def kernel(
    slabs,
    leaves,
    count_s,
    points_h,
    targets_h,
    columns_h,
    right_h,
    left_h,
    basis_h,
    transfer_h,
    lift_h,
    coupling_h,
    apex_h,
    near_h,
    product_ref,
    adjoint_ref,
    right_v,
    left_v,
    basis_v,
    transfer_v,
    lift_v,
    coupling_v,
    apex_v,
    near_v,
    columns_v,
    table_v,
    far_table_v,
    points_s,
    targets_s,
    table_s,
    far_table_s,
    ext_v,
    masked_left_v,
    leaf_v,
    transfer2_v,
    lift2_v,
    coupling2_v,
    apex2_v,
    collected_v,
    near_out_v,
    edge_out_v,
    edge_in_v,
    share_v,
    share_in_v,
    slab_v,
    top_v,
    parents_v,
    terms_v,
    core_out_v,
    core_in_v,
    slab_out_v,
    slab_in_v,
    own_v,
    chip_out_v,
    chip_in_v,
    in_sem,
    table_sem,
    halo_send,
    halo_recv,
    edge_send,
    edge_recv,
    share_send,
    share_recv,
    slab_send,
    slab_recv,
    top_send,
    top_recv,
    pchip_send,
    pchip_recv,
    pslab_send,
    pslab_recv,
    ochip_send,
    ochip_recv,
    oslab_send,
    oslab_recv,
    core_send,
    core_recv,
):
    rhs = right_h.shape[0]
    slots, clusters = columns_v.shape
    rank = leaf_v.shape[1] // clusters
    pack = B // rank
    far_slots = coupling_v.shape[0]
    devices = slabs * leaves
    chips = leaves // CORES
    group = slabs * chips
    width = 2 * HW + 1
    chunk = share_v.shape[1]
    my_slab = lax.axis_index("slab")
    my_leaf = lax.axis_index("leaf")
    my_chip = my_leaf // CORES
    my_core = my_leaf % CORES
    me = my_slab * leaves + my_leaf
    first = 1 - (me + devices - 1) // devices
    last = (me + 1) // devices
    is_right = my_leaf * chunk < rhs

    def place(d):
        return (d // leaves, d % leaves)

    def loop(low, high, act):
        def step(k, carry):
            act(k)
            return carry

        lax.fori_loop(low, high, step, 0)

    inputs = [
        pltpu.make_async_copy(src, dst, in_sem.at[i])
        for i, (src, dst) in enumerate(
            [
                (right_h, right_v),
                (left_h, left_v),
                (basis_h, basis_v),
                (transfer_h, transfer_v),
                (lift_h, lift_v),
                (coupling_h, coupling_v),
                (near_h, near_v.at[pl.ds(0, clusters * slots)]),
                (columns_h, columns_v),
                (points_h, points_s),
                (targets_h, targets_s),
            ]
        )
    ]
    apex_row = pltpu.make_async_copy(apex_h.at[my_slab], apex_v, in_sem.at[10])
    apex_column = pltpu.make_async_copy(apex_h.at[:, my_slab], apex_v, in_sem.at[10])
    for copy in inputs[7:] + inputs[:7]:
        copy.start()

    @pl.when(is_right)
    def _():
        apex_row.start()

    @pl.when(jnp.logical_not(is_right))
    def _():
        apex_column.start()

    ext_v[0:HW] = jnp.zeros((HW, rhs, B), BF)
    ext_v[clusters + HW :] = jnp.zeros((HW, rhs, B), BF)
    edge_in_v[...] = jnp.zeros_like(edge_in_v)
    slab_in_v[my_slab] = jnp.zeros(slab_in_v.shape[1:], BF)
    chip_in_v[my_chip] = jnp.zeros(chip_in_v.shape[1:], BF)
    parents_v[CORES * group] = jnp.zeros(parents_v.shape[1:], BF)

    barrier = pltpu.get_barrier_semaphore()

    def greet(slab, leaf):
        pl.semaphore_signal(barrier, inc=1, device_id=(slab, leaf), device_id_type=MESH)

    loop(1, leaves, lambda k: greet(my_slab, (my_leaf + k) % leaves))
    loop(1, slabs, lambda k: greet((my_slab + k) % slabs, my_leaf))
    after = jnp.where(my_leaf == leaves - 1, jnp.where(my_slab < slabs - 1, 1, 0), 0)
    before = jnp.where(my_leaf == 0, jnp.where(my_slab > 0, 1, 0), 0)

    @pl.when(after == 1)
    def _():
        greet(my_slab + 1, 0)

    @pl.when(before == 1)
    def _():
        greet(my_slab - 1, leaves - 1)

    collected_v[...] = jnp.zeros_like(collected_v)
    near_v[clusters * slots] = jnp.zeros((B, B), BF)
    terms_v[far_slots] = jnp.zeros(terms_v.shape[1:], F32)

    for copy in inputs[7:]:
        copy.wait()
    row = lax.broadcasted_iota(jnp.int32, (1, clusters), 1)
    opening = (
        row
        + first * jnp.maximum(HW - row, 0)
        - last * jnp.maximum(row - (clusters - HW - 1), 0)
    )
    spots = [columns_v[s : s + 1] - (me * clusters - HW) for s in range(slots)]
    for w in range(width):
        found = jnp.full((1, clusters), clusters * slots, jnp.int32)
        for s in range(slots):
            found = jnp.where(spots[s] == opening + w, row * slots + s, found)
        table_v[w : w + 1] = found
    for s in range(slots):
        table_v[width + s : width + s + 1] = jnp.clip(spots[s], 0, clusters + 2 * HW - 1)
    owner = lax.broadcasted_iota(jnp.int32, (1, devices), 1)
    found = jnp.full((1, devices), far_slots, jnp.int32)
    for f in range(far_slots):
        target = jnp.where(f < count_s[0], targets_s[f], -1)
        found = jnp.where(owner == target, f, found)
    far_table_v[0:1] = found
    tables = [
        pltpu.make_async_copy(table_v, table_s, table_sem.at[0]),
        pltpu.make_async_copy(far_table_v, far_table_s, table_sem.at[1]),
    ]
    for copy in tables:
        copy.start()

    lane = lax.broadcasted_iota(jnp.int32, (rhs, B), 1)
    lane2 = lax.broadcasted_iota(jnp.int32, (2 * rhs, B), 1)

    for copy in inputs[:3]:
        copy.wait()

    def leaf_step(g):
        rows = []
        for u in range(pack):
            c = g * pack + u
            window = slice(c * B, (c + 1) * B)
            mask = jnp.where(lane < points_s[c], 1.0, 0.0).astype(BF)
            r = right_v[:, window] * mask
            l = left_v[:, window] * mask
            ext_v[c + HW] = r
            masked_left_v[c] = l
            rows += [r, l]
        both = nt(jnp.concatenate(rows, axis=0), basis_v[g])
        leaf = both[: 2 * rhs]
        for u in range(1, pack):
            leaf = jnp.where(lane2 < u * rank, leaf, both[2 * rhs * u : 2 * rhs * (u + 1)])
        high, low = split(leaf)
        leaf_v[: 2 * rhs, g * B : (g + 1) * B] = high
        leaf_v[2 * rhs :, g * B : (g + 1) * B] = low

    for g in range(clusters // pack):
        leaf_step(g)
    inputs[3].wait()
    inputs[4].wait()
    transfer2_v[...] = wide(transfer_v[...])
    lift2_v[...] = wide(lift_v[...])
    both = nn(leaf_v[...], transfer2_v[...])
    k2 = transfer_v.shape[1]
    parent = both[: 2 * rhs, :k2] + both[2 * rhs :, :k2] + both[: 2 * rhs, k2:]

    def spot(slab, leaf):
        return (leaf % CORES) * group + slab * chips + leaf // CORES

    parents_v[spot(my_slab, my_leaf)] = parent[:rhs].astype(BF)
    share = three_nn(parent, lift2_v[...])
    for j in range(leaves):
        share_v[j] = share[j * chunk : (j + 1) * chunk]

    pl.semaphore_wait(barrier, leaves - 1 + slabs - 1 + after + before)

    def remote(src, dst, send, recv, device):
        return pltpu.make_async_remote_copy(
            src_ref=src,
            dst_ref=dst,
            send_sem=send,
            recv_sem=recv,
            device_id=device,
            device_id_type=MESH,
        )

    def share_copy(k):
        peer = (my_leaf + k) % leaves
        return remote(
            share_v.at[peer],
            share_in_v.at[my_leaf],
            share_send.at[k],
            share_recv.at[k],
            (my_slab, peer),
        )

    def share_arrival(k):
        peer = (my_leaf + leaves - k) % leaves
        return remote(
            share_v.at[my_leaf],
            share_in_v.at[peer],
            share_send.at[k],
            share_recv.at[k],
            (my_slab, peer),
        )

    def slab_copy(k):
        return remote(
            slab_v.at[my_slab],
            slab_v.at[my_slab],
            slab_send.at[k],
            slab_recv.at[k],
            ((my_slab + k) % slabs, my_leaf),
        )

    def slab_arrival(k):
        peer = (my_slab + slabs - k) % slabs
        return remote(
            slab_v.at[my_slab],
            slab_v.at[peer],
            slab_send.at[k],
            slab_recv.at[k],
            (peer, my_leaf),
        )

    def top_copy(k):
        return remote(
            top_v.at[my_leaf],
            top_v.at[my_leaf],
            top_send.at[k],
            top_recv.at[k],
            (my_slab, (my_leaf + k) % leaves),
        )

    def top_arrival(k):
        peer = (my_leaf + leaves - k) % leaves
        return remote(
            top_v.at[my_leaf],
            top_v.at[peer],
            top_send.at[k],
            top_recv.at[k],
            (my_slab, peer),
        )

    def chip_leaf(k):
        return ((my_chip + k) % chips) * CORES + my_core

    def parent_chip_copy(k):
        at = spot(my_slab, my_leaf)
        return remote(
            parents_v.at[at],
            parents_v.at[at],
            pchip_send.at[k],
            pchip_recv.at[k],
            (my_slab, chip_leaf(k)),
        )

    def parent_chip_arrival(k):
        leaf = chip_leaf(chips - k)
        return remote(
            parents_v.at[spot(my_slab, my_leaf)],
            parents_v.at[spot(my_slab, leaf)],
            pchip_send.at[k],
            pchip_recv.at[k],
            (my_slab, leaf),
        )

    def column(core, slab):
        return parents_v.at[pl.ds(core * group + slab * chips, chips)]

    def parent_slab_copy(k):
        return remote(
            column(my_core, my_slab),
            column(my_core, my_slab),
            pslab_send.at[k],
            pslab_recv.at[k],
            ((my_slab + k) % slabs, my_leaf),
        )

    def parent_slab_arrival(k):
        peer = (my_slab + slabs - k) % slabs
        return remote(
            column(my_core, my_slab),
            column(my_core, peer),
            pslab_send.at[k],
            pslab_recv.at[k],
            (peer, my_leaf),
        )

    partner = (my_slab, my_chip * CORES + 1 - my_core)

    def parent_core_copy():
        half = parents_v.at[pl.ds(my_core * group, group)]
        return remote(half, half, core_send.at[0], core_recv.at[0], partner)

    def parent_core_arrival():
        half = parents_v.at[pl.ds(my_core * group, group)]
        other = parents_v.at[pl.ds((1 - my_core) * group, group)]
        return remote(half, other, core_send.at[0], core_recv.at[0], partner)

    def outward_core_copy():
        return remote(core_out_v, core_in_v, core_send.at[1], core_recv.at[1], partner)

    def outward_slab_copy(k):
        peer = (my_slab + k) % slabs
        return remote(
            slab_out_v.at[peer],
            slab_in_v.at[my_slab],
            oslab_send.at[k],
            oslab_recv.at[k],
            (peer, my_leaf),
        )

    def outward_slab_arrival(k):
        peer = (my_slab + slabs - k) % slabs
        return remote(
            slab_out_v.at[my_slab],
            slab_in_v.at[peer],
            oslab_send.at[k],
            oslab_recv.at[k],
            (peer, my_leaf),
        )

    def outward_chip_copy(k):
        peer = (my_chip + k) % chips
        return remote(
            chip_out_v.at[peer],
            chip_in_v.at[my_chip],
            ochip_send.at[k],
            ochip_recv.at[k],
            (my_slab, chip_leaf(k)),
        )

    def outward_chip_arrival(k):
        peer = (my_chip + chips - k) % chips
        return remote(
            chip_out_v.at[my_chip],
            chip_in_v.at[peer],
            ochip_send.at[k],
            ochip_recv.at[k],
            (my_slab, chip_leaf(chips - k)),
        )

    def halo_copy(to_next):
        where = me + 1 if to_next else me - 1
        src = clusters if to_next else HW
        dst = 0 if to_next else clusters + HW
        i = 0 if to_next else 1
        return remote(
            ext_v.at[pl.ds(src, HW)],
            ext_v.at[pl.ds(dst, HW)],
            halo_send.at[i],
            halo_recv.at[i],
            place(where),
        )

    def edge_copy(to_next):
        i = 1 if to_next else 0
        return remote(
            edge_out_v.at[i],
            edge_in_v.at[i],
            edge_send.at[i],
            edge_recv.at[i],
            place(me + 1 if to_next else me - 1),
        )

    loop(1, leaves, lambda k: share_copy(k).start())
    loop(1, chips, lambda k: parent_chip_copy(k).start())
    share_in_v[my_leaf] = share_v[my_leaf]

    @pl.when(me < devices - 1)
    def _():
        halo_copy(True).start()

    @pl.when(me > 0)
    def _():
        halo_copy(False).start()

    inputs[5].wait()
    left_both = stacked(parent[rhs:])

    def term(f):
        pair = wide(coupling_v[f])
        coupling2_v[f] = pair
        both = nn(left_both, pair)
        terms_v[f] = both[:rhs, :k2] + both[rhs:, :k2] + both[:rhs, k2:]

    unroll = 4

    def term_group(g):
        for u in range(unroll):
            term(g * unroll + u)

    loop(0, far_slots // unroll, term_group)
    for copy in tables:
        copy.wait()

    def owned(slab, chip, core):
        return terms_v[far_table_s[0, slab * leaves + chip * CORES + core]]

    def core_group(slab):
        for chip in range(chips):
            core_out_v[slab * chips + chip] = owned(slab, chip, 1 - my_core)

    for slab in range(slabs):
        core_group(slab)
    outward_core_copy().start()

    apex_row.wait()
    for t in range(slabs):
        apex2_v[t] = wide(apex_v[t])

    inputs[6].wait()

    def near_back(i, e0):
        left = masked_left_v[i]
        for w in range(width):
            collected_v[e0 + w] += nn(left, near_v[table_s[w, i]])

    def near_forward(i):
        blocks = jnp.concatenate([near_v[i * slots + s] for s in range(slots)], axis=1)
        picked = jnp.concatenate([ext_v[table_s[width + s, i]] for s in range(slots)], axis=1)
        near_out_v[i] = nt(picked, blocks)

    for i in range(HW):
        near_back(i, i + first * (HW - i))
    for i in range(clusters - HW, clusters):
        near_back(i, i - last * (i - (clusters - HW - 1)))

    edge_out_v[0] = collected_v[0:HW].astype(BF)
    edge_out_v[1] = collected_v[clusters + HW :].astype(BF)

    loop(1, leaves, lambda k: share_arrival(k).wait_recv())
    total = share_in_v[0]
    for j in range(1, leaves):
        total = total + share_in_v[j]
    slab_v[my_slab] = total
    loop(1, slabs, lambda k: slab_copy(k).start())

    outward_core_copy().wait_recv()
    for slab in range(slabs):
        for chip in range(chips):
            k = slab * chips + chip
            slab_out_v[slab, chip] = (owned(slab, chip, my_core) + core_in_v[k]).astype(BF)
    loop(1, slabs, lambda k: outward_slab_copy(k).start())
    for chip in range(chips):
        own_v[chip] = owned(my_slab, chip, my_core) + core_in_v[my_slab * chips + chip]

    loop(1, chips, lambda k: parent_chip_arrival(k).wait_recv())
    loop(1, slabs, lambda k: parent_slab_copy(k).start())

    @pl.when(me < devices - 1)
    def _():
        edge_copy(True).start()

    @pl.when(me > 0)
    def _():
        edge_copy(False).start()

    def middle_back(g):
        i = HW + g * HW
        lefts = [masked_left_v[i + u] for u in range(HW)]
        for e in range(width + HW - 1):
            rows = [u for u in range(HW) if 0 <= e - u < width]
            left = jnp.concatenate([lefts[u] for u in rows], axis=1)
            blocks = jnp.concatenate([near_v[table_s[e - u, i + u]] for u in rows], axis=0)
            collected_v[i + e] += nn(left, blocks)

    middles = (clusters - 2 * HW) // HW
    loop(0, middles // 2, middle_back)

    loop(1, slabs, lambda k: slab_arrival(k).wait_recv())

    def apex_products(product):
        total = jnp.zeros((chunk, lift_v.shape[1]), F32)
        for t in range(slabs):
            other = jnp.where(my_slab == t, 0.0, 1.0)
            total += product(slab_v[t] * other, apex2_v[t])
        top_v[my_leaf] = total

    @pl.when(is_right)
    def _():
        apex_products(three_nt)

    @pl.when(jnp.logical_not(is_right))
    def _():
        apex_products(three_nn)

    loop(1, leaves, lambda k: top_copy(k).start())

    loop(1, slabs, lambda k: outward_slab_arrival(k).wait_recv())
    for chip in range(chips):
        total = own_v[chip]
        for t in range(slabs):
            total = total + slab_in_v[t, chip].astype(F32)
        own_v[chip] = total
        chip_out_v[chip] = total.astype(BF)
    loop(1, chips, lambda k: outward_chip_copy(k).start())

    loop(1, slabs, lambda k: parent_slab_arrival(k).wait_recv())
    parent_core_copy().start()

    loop(middles // 2, middles, middle_back)

    @pl.when(me > 0)
    def _():
        halo_copy(True).wait_recv()

    @pl.when(me < devices - 1)
    def _():
        halo_copy(False).wait_recv()

    def forward_group(g):
        for u in range(HW):
            near_forward(g * HW + u)

    loop(0, clusters // HW, forward_group)

    @pl.when(me > 0)
    def _():
        edge_copy(True).wait_recv()

    @pl.when(me < devices - 1)
    def _():
        edge_copy(False).wait_recv()

    collected_v[HW : 2 * HW] += edge_in_v[1].astype(F32)
    collected_v[clusters : clusters + HW] += edge_in_v[0].astype(F32)

    parent_core_arrival().wait_recv()
    batch = 4
    far_right = jnp.zeros((rhs, k2), F32)

    def far_group(g, total):
        chosen, pairs = [], []
        for u in range(batch):
            f = g * batch + u
            target = targets_s[f]
            at = spot(target // leaves, target % leaves)
            row = parents_v[jnp.where(f < count_s[0], at, CORES * group)]
            chosen += [row, row]
            pairs.append(coupling2_v[f])
        return total + nt(jnp.concatenate(chosen, axis=1), jnp.concatenate(pairs, axis=1))

    far_right = lax.fori_loop(0, far_slots // batch, far_group, far_right)

    loop(1, chips, lambda k: outward_chip_arrival(k).wait_recv())
    far_left = own_v[my_chip]
    for chip in range(chips):
        far_left = far_left + chip_in_v[chip].astype(F32)

    loop(1, leaves, lambda k: top_arrival(k).wait_recv())
    top = jnp.concatenate([top_v[j] for j in range(leaves)], axis=0)
    hat = three_nt(top, lift2_v[...]) + jnp.concatenate([far_right, far_left], axis=0)
    hat2 = paired_rows(hat)
    span = 2 * B
    for n in range(clusters * rank // span):
        both = nt(hat2, transfer2_v[n * span : (n + 1) * span])
        down = (both[: 2 * rhs] + both[2 * rhs :]).astype(BF)
        for h in range(span // B):
            g = n * (span // B) + h
            piece = down[:, h * B : (h + 1) * B]
            rows = [
                jnp.where((lane2 >= u * rank) & (lane2 < (u + 1) * rank), piece, jnp.zeros_like(piece))
                for u in range(pack)
            ]
            out = nn(jnp.concatenate(rows, axis=0), basis_v[g])
            for u in range(pack):
                c = g * pack + u
                keep = lane < points_s[c]
                base = 2 * rhs * u
                window = slice(c * B, (c + 1) * B)
                product_ref[:, window] = jnp.where(
                    keep, near_out_v[c] + out[base : base + rhs], 0.0
                )
                adjoint_ref[:, window] = jnp.where(
                    keep, collected_v[c + HW] + out[base + rhs : base + 2 * rhs], 0.0
                )

    loop(1, leaves, lambda k: share_copy(k).wait_send())
    loop(1, leaves, lambda k: top_copy(k).wait_send())
    loop(1, slabs, lambda k: slab_copy(k).wait_send())
    loop(1, slabs, lambda k: parent_slab_copy(k).wait_send())
    loop(1, slabs, lambda k: outward_slab_copy(k).wait_send())
    loop(1, chips, lambda k: parent_chip_copy(k).wait_send())
    loop(1, chips, lambda k: outward_chip_copy(k).wait_send())
    parent_core_copy().wait_send()
    outward_core_copy().wait_send()

    @pl.when(me < devices - 1)
    def _():
        halo_copy(True).wait_send()
        edge_copy(True).wait_send()

    @pl.when(me > 0)
    def _():
        halo_copy(False).wait_send()
        edge_copy(False).wait_send()


def shards(
    right_sides,
    left_sides,
    near_blocks,
    near_columns,
    cluster_points,
    leaf_basis,
    transfer,
    far_parents,
    far_count,
    coupling,
    slab_transfer,
    apex_coupling,
):
    slabs, leaves = lax.axis_size("slab"), lax.axis_size("leaf")
    devices = slabs * leaves
    chips = leaves // CORES
    group = slabs * chips
    rhs, columns = right_sides.shape
    clusters, slots = near_columns.shape
    rank, k2 = transfer.shape[1:]
    k3 = slab_transfer.shape[2]
    far_slots = coupling.shape[1]
    width = 2 * HW + 1
    chunk = 2 * rhs // leaves
    pack = B // rank
    hbm = pl.BlockSpec(memory_space=pltpu.HBM)
    vmem = pl.BlockSpec(memory_space=pltpu.VMEM)
    dma = pltpu.SemaphoreType.DMA
    out = jax.ShapeDtypeStruct((rhs, columns), F32)
    return pl.pallas_call(
        functools.partial(kernel, slabs, leaves),
        out_shape=(out, out),
        in_specs=[pl.BlockSpec(memory_space=pltpu.SMEM)] + [hbm] * 11,
        out_specs=(vmem, vmem),
        scratch_shapes=[
            pltpu.VMEM((rhs, columns), BF),
            pltpu.VMEM((rhs, columns), BF),
            pltpu.VMEM((clusters // pack, B, B), BF),
            pltpu.VMEM((clusters * rank, k2), F32),
            pltpu.VMEM((k2, k3), F32),
            pltpu.VMEM(coupling.shape[1:], F32),
            pltpu.VMEM((slabs, k3, k3), F32),
            pltpu.VMEM((clusters * slots + 1, B, B), BF),
            pltpu.VMEM((slots, clusters), jnp.int32),
            pltpu.VMEM((width + slots, clusters), jnp.int32),
            pltpu.VMEM((1, devices), jnp.int32),
            pltpu.SMEM((clusters,), jnp.int32),
            pltpu.SMEM((far_slots,), jnp.int32),
            pltpu.SMEM((width + slots, clusters), jnp.int32),
            pltpu.SMEM((1, devices), jnp.int32),
            pltpu.VMEM((clusters + 2 * HW, rhs, B), BF),
            pltpu.VMEM((clusters, rhs, B), BF),
            pltpu.VMEM((4 * rhs, clusters * rank), BF),
            pltpu.VMEM((clusters * rank, 2 * k2), BF),
            pltpu.VMEM((k2, 2 * k3), BF),
            pltpu.VMEM((far_slots, k2, 2 * k2), BF),
            pltpu.VMEM((slabs, k3, 2 * k3), BF),
            pltpu.VMEM((clusters + 2 * HW, rhs, B), F32),
            pltpu.VMEM((clusters, rhs, B), F32),
            pltpu.VMEM((2, HW, rhs, B), BF),
            pltpu.VMEM((2, HW, rhs, B), BF),
            pltpu.VMEM((leaves, chunk, k3), F32),
            pltpu.VMEM((leaves, chunk, k3), F32),
            pltpu.VMEM((slabs, chunk, k3), F32),
            pltpu.VMEM((leaves, chunk, k3), F32),
            pltpu.VMEM((CORES * group + 1, rhs, k2), BF),
            pltpu.VMEM((far_slots + 1, rhs, k2), F32),
            pltpu.VMEM((group, rhs, k2), F32),
            pltpu.VMEM((group, rhs, k2), F32),
            pltpu.VMEM((slabs, chips, rhs, k2), BF),
            pltpu.VMEM((slabs, chips, rhs, k2), BF),
            pltpu.VMEM((chips, rhs, k2), F32),
            pltpu.VMEM((chips, rhs, k2), BF),
            pltpu.VMEM((chips, rhs, k2), BF),
            dma((11,)),
            dma((2,)),
            dma((2,)),
            dma((2,)),
            dma((2,)),
            dma((2,)),
            dma((leaves,)),
            dma((leaves,)),
            dma((slabs,)),
            dma((slabs,)),
            dma((leaves,)),
            dma((leaves,)),
            dma((chips,)),
            dma((chips,)),
            dma((slabs,)),
            dma((slabs,)),
            dma((chips,)),
            dma((chips,)),
            dma((slabs,)),
            dma((slabs,)),
            dma((2,)),
            dma((2,)),
        ],
        compiler_params=pltpu.CompilerParams(
            collective_id=0, has_side_effects=True, vmem_limit_bytes=50 * 1024 * 1024
        ),
        name="h2_step",
    )(
        far_count,
        *[
            pltpu.with_memory_space_constraint(array, pltpu.HBM)
            for array in (
                cluster_points,
                far_parents[0],
                near_columns.T,
                right_sides,
                left_sides,
                leaf_basis.reshape(clusters // pack, B, B),
                transfer.reshape(clusters * rank, k2),
                slab_transfer[0],
                coupling[0],
                apex_coupling,
                near_blocks.reshape(-1, B, B),
            )
        ],
    )


def solution(mesh):
    return jax.shard_map(
        shards,
        mesh=mesh,
        in_specs=(
            P(None, ("slab", "leaf")),
            P(None, ("slab", "leaf")),
            P(("slab", "leaf"), None, None, None),
            P(("slab", "leaf"), None),
            P(("slab", "leaf")),
            P(("slab", "leaf"), None, None),
            P(("slab", "leaf"), None, None),
            P(("slab", "leaf"), None),
            P(("slab", "leaf")),
            P(("slab", "leaf"), None, None, None),
            P(("slab", "leaf"), None, None),
            P(),
        ),
        out_specs=(P(None, ("slab", "leaf")), P(None, ("slab", "leaf"))),
        check_vma=False,
    )
```

time: 40.2 us -> 26.4 us (0.66)
  Pallas kernels: 38.8 us -> 23.4 us
  local copies, waits for them, and re-layouts: 0 us -> 1.59 us
    pallas_call x2 -> x1, Pallas kernels: 38.8 us -> 23.4 us  [shards(): pl.pallas_call(functools.partial(kernel, slabs, leaves), out_shape=(out,...]
    unnamed x0 -> x2, local copies, waits for them, and re-layouts: none -> 1.59 us
where the time goes in v1:
time: 26.4 us; the launch traced here: 26.2 us
  Pallas kernels  23.4 us (89%)
  local copies, waits for them, and re-layouts  1.59 us (6%)
  between operations  1.29 us (5%)
    pallas_call x1, Pallas kernels, shards(): pl.pallas_call(functools.partial(kernel, slabs, leaves), out_shape=(out,...  23.4 us
    unnamed x2, local copies, waits for them, and re-layouts  1.59 us

profile of v1, /device:TPU:0, one launch (start us, length us, event | category | flops | bytes accessed | tf_op | source)
XLA Modules:
  0.0 26.2 jit_solution(7654788097895931981)
XLA Ops:
  1.3 23.4 %h2_step.1 = (f32[32,4096]{1,0:T(8,128)S(1)}, f32[32,4096]{1,0:T(8,128)S(1)}) custom-call(s32[1]{0:T(128)S(6)} %copy.16.count_s, s32[32]{0:T(128)} %points_h.1, s32[24]{0:T(128)} %bitcast.13, s32[8,32]{1,0:T(8,128)} %bitcast.12, bf16[32,4096]{1,0:T(8,128)(2,1)} %right_h.1, bf16[32,4096]{1,0:T(8,128)(2,1)} %left_h.1, bf16[16,128,128]{2,1,0:T(8,128)(2,1)} %bitcast.10, ...), custom_call_target="tpu_custom_call" | custom-call | tf_op jit(solution)/shard_map/h2_step/pallas_call | solution.py:757
  24.6 0.8 %copy.17 = f32[32,4096]{1,0:T(8,128)} copy(f32[32,4096]{1,0:T(8,128)S(1)} %get-tuple-element.4) | data formatting | bytes 1048576
  25.4 0.8 %copy.18 = f32[32,4096]{1,0:T(8,128)} copy(f32[32,4096]{1,0:T(8,128)S(1)} %get-tuple-element.5) | data formatting | bytes 1048576

commit v2 on v1

--- a/solution.py
+++ b/solution.py
@@ -74,11 +74,14 @@
     coupling_h,
     apex_h,
     near_h,
-    product_ref,
-    adjoint_ref,
+    hat_ref,
+    near_out_v,
+    collected_v,
+    transfer2_v,
+    basis_v,
+    keep_v,
     right_v,
     left_v,
-    basis_v,
     transfer_v,
     lift_v,
     coupling_v,
@@ -94,12 +97,9 @@
     ext_v,
     masked_left_v,
     leaf_v,
-    transfer2_v,
     lift2_v,
     coupling2_v,
     apex2_v,
-    collected_v,
-    near_out_v,
     edge_out_v,
     edge_in_v,
     share_v,
@@ -186,7 +186,7 @@
     ]
     apex_row = pltpu.make_async_copy(apex_h.at[my_slab], apex_v, in_sem.at[10])
     apex_column = pltpu.make_async_copy(apex_h.at[:, my_slab], apex_v, in_sem.at[10])
-    for copy in inputs[7:] + inputs[:7]:
+    for copy in inputs[7:] + inputs[:6]:
         copy.start()
 
     @pl.when(is_right)
@@ -222,12 +222,251 @@
     def _():
         greet(my_slab - 1, leaves - 1)
 
+    lane = lax.broadcasted_iota(jnp.int32, (rhs, B), 1)
+    lane2 = lax.broadcasted_iota(jnp.int32, (2 * rhs, B), 1)
+
+    for copy in inputs[8:] + inputs[:4]:
+        copy.wait()
+
+    def leaf_step(g):
+        rows = []
+        for u in range(pack):
+            c = g * pack + u
+            window = slice(c * B, (c + 1) * B)
+            mask = jnp.where(lane < points_s[c], 1.0, 0.0).astype(BF)
+            keep_v[c : c + 1] = jnp.where(lane[:1] < points_s[c], 1.0, 0.0)
+            r = right_v[:, window] * mask
+            l = left_v[:, window] * mask
+            ext_v[c + HW] = r
+            masked_left_v[c] = l
+            rows += [r, l]
+        both = nt(jnp.concatenate(rows, axis=0), basis_v[g])
+        leaf = both[: 2 * rhs]
+        for u in range(1, pack):
+            leaf = jnp.where(lane2 < u * rank, leaf, both[2 * rhs * u : 2 * rhs * (u + 1)])
+        high, low = split(leaf)
+        leaf_v[: 2 * rhs, g * B : (g + 1) * B] = high
+        leaf_v[2 * rhs :, g * B : (g + 1) * B] = low
+
+    inputs[6].start()
+    for g in range(clusters // pack):
+        leaf_step(g)
+    inputs[4].wait()
+    transfer2_v[...] = wide(transfer_v[...])
+    lift2_v[...] = wide(lift_v[...])
+    both = nn(leaf_v[...], transfer2_v[...])
+    k2 = transfer_v.shape[1]
+    parent = both[: 2 * rhs, :k2] + both[2 * rhs :, :k2] + both[: 2 * rhs, k2:]
+
+    def spot(slab, leaf):
+        return (leaf % CORES) * group + slab * chips + leaf // CORES
+
+    parents_v[spot(my_slab, my_leaf)] = parent[:rhs].astype(BF)
+    share = three_nn(parent, lift2_v[...])
+    for j in range(leaves):
+        share_v[j] = share[j * chunk : (j + 1) * chunk]
+
+    pl.semaphore_wait(barrier, leaves - 1 + slabs - 1 + after + before)
+
+    def remote(src, dst, send, recv, device):
+        return pltpu.make_async_remote_copy(
+            src_ref=src,
+            dst_ref=dst,
+            send_sem=send,
+            recv_sem=recv,
+            device_id=device,
+            device_id_type=MESH,
+        )
+
+    def share_copy(k):
+        peer = (my_leaf + k) % leaves
+        return remote(
+            share_v.at[peer],
+            share_in_v.at[my_leaf],
+            share_send.at[k],
+            share_recv.at[k],
+            (my_slab, peer),
+        )
+
+    def share_arrival(k):
+        peer = (my_leaf + leaves - k) % leaves
+        return remote(
+            share_v.at[my_leaf],
+            share_in_v.at[peer],
+            share_send.at[k],
+            share_recv.at[k],
+            (my_slab, peer),
+        )
+
+    def slab_copy(k):
+        return remote(
+            slab_v.at[my_slab],
+            slab_v.at[my_slab],
+            slab_send.at[k],
+            slab_recv.at[k],
+            ((my_slab + k) % slabs, my_leaf),
+        )
+
+    def slab_arrival(k):
+        peer = (my_slab + slabs - k) % slabs
+        return remote(
+            slab_v.at[my_slab],
+            slab_v.at[peer],
+            slab_send.at[k],
+            slab_recv.at[k],
+            (peer, my_leaf),
+        )
+
+    def top_copy(k):
+        return remote(
+            top_v.at[my_leaf],
+            top_v.at[my_leaf],
+            top_send.at[k],
+            top_recv.at[k],
+            (my_slab, (my_leaf + k) % leaves),
+        )
+
+    def top_arrival(k):
+        peer = (my_leaf + leaves - k) % leaves
+        return remote(
+            top_v.at[my_leaf],
+            top_v.at[peer],
+            top_send.at[k],
+            top_recv.at[k],
+            (my_slab, peer),
+        )
+
+    def chip_leaf(k):
+        return ((my_chip + k) % chips) * CORES + my_core
+
+    def parent_chip_copy(k):
+        at = spot(my_slab, my_leaf)
+        return remote(
+            parents_v.at[at],
+            parents_v.at[at],
+            pchip_send.at[k],
+            pchip_recv.at[k],
+            (my_slab, chip_leaf(k)),
+        )
+
+    def parent_chip_arrival(k):
+        leaf = chip_leaf(chips - k)
+        return remote(
+            parents_v.at[spot(my_slab, my_leaf)],
+            parents_v.at[spot(my_slab, leaf)],
+            pchip_send.at[k],
+            pchip_recv.at[k],
+            (my_slab, leaf),
+        )
+
+    def column(core, slab):
+        return parents_v.at[pl.ds(core * group + slab * chips, chips)]
+
+    def parent_slab_copy(k):
+        return remote(
+            column(my_core, my_slab),
+            column(my_core, my_slab),
+            pslab_send.at[k],
+            pslab_recv.at[k],
+            ((my_slab + k) % slabs, my_leaf),
+        )
+
+    def parent_slab_arrival(k):
+        peer = (my_slab + slabs - k) % slabs
+        return remote(
+            column(my_core, my_slab),
+            column(my_core, peer),
+            pslab_send.at[k],
+            pslab_recv.at[k],
+            (peer, my_leaf),
+        )
+
+    partner = (my_slab, my_chip * CORES + 1 - my_core)
+
+    def parent_core_copy():
+        half = parents_v.at[pl.ds(my_core * group, group)]
+        return remote(half, half, core_send.at[0], core_recv.at[0], partner)
+
+    def parent_core_arrival():
+        half = parents_v.at[pl.ds(my_core * group, group)]
+        other = parents_v.at[pl.ds((1 - my_core) * group, group)]
+        return remote(half, other, core_send.at[0], core_recv.at[0], partner)
+
+    def outward_core_copy():
+        return remote(core_out_v, core_in_v, core_send.at[1], core_recv.at[1], partner)
+
+    def outward_slab_copy(k):
+        peer = (my_slab + k) % slabs
+        return remote(
+            slab_out_v.at[peer],
+            slab_in_v.at[my_slab],
+            oslab_send.at[k],
+            oslab_recv.at[k],
+            (peer, my_leaf),
+        )
+
+    def outward_slab_arrival(k):
+        peer = (my_slab + slabs - k) % slabs
+        return remote(
+            slab_out_v.at[my_slab],
+            slab_in_v.at[peer],
+            oslab_send.at[k],
+            oslab_recv.at[k],
+            (peer, my_leaf),
+        )
+
+    def outward_chip_copy(k):
+        peer = (my_chip + k) % chips
+        return remote(
+            chip_out_v.at[peer],
+            chip_in_v.at[my_chip],
+            ochip_send.at[k],
+            ochip_recv.at[k],
+            (my_slab, chip_leaf(k)),
+        )
+
+    def outward_chip_arrival(k):
+        peer = (my_chip + chips - k) % chips
+        return remote(
+            chip_out_v.at[my_chip],
+            chip_in_v.at[peer],
+            ochip_send.at[k],
+            ochip_recv.at[k],
+            (my_slab, chip_leaf(chips - k)),
+        )
+
+    def halo_copy(to_next):
+        where = me + 1 if to_next else me - 1
+        src = clusters if to_next else HW
+        dst = 0 if to_next else clusters + HW
+        i = 0 if to_next else 1
+        return remote(
+            ext_v.at[pl.ds(src, HW)],
+            ext_v.at[pl.ds(dst, HW)],
+            halo_send.at[i],
+            halo_recv.at[i],
+            place(where),
+        )
+
+    def edge_copy(to_next):
+        i = 1 if to_next else 0
+        return remote(
+            edge_out_v.at[i],
+            edge_in_v.at[i],
+            edge_send.at[i],
+            edge_recv.at[i],
+            place(me + 1 if to_next else me - 1),
+        )
+
+    loop(1, leaves, lambda k: share_copy(k).start())
+    loop(1, chips, lambda k: parent_chip_copy(k).start())
+    share_in_v[my_leaf] = share_v[my_leaf]
+
     collected_v[...] = jnp.zeros_like(collected_v)
     near_v[clusters * slots] = jnp.zeros((B, B), BF)
     terms_v[far_slots] = jnp.zeros(terms_v.shape[1:], F32)
 
-    for copy in inputs[7:]:
-        copy.wait()
+    inputs[7].wait()
     row = lax.broadcasted_iota(jnp.int32, (1, clusters), 1)
     opening = (
         row
@@ -255,253 +494,6 @@
     for copy in tables:
         copy.start()
 
-    lane = lax.broadcasted_iota(jnp.int32, (rhs, B), 1)
-    lane2 = lax.broadcasted_iota(jnp.int32, (2 * rhs, B), 1)
-
-    for copy in inputs[:3]:
-        copy.wait()
-
-    def leaf_step(g):
-        rows = []
-        for u in range(pack):
-            c = g * pack + u
-            window = slice(c * B, (c + 1) * B)
-            mask = jnp.where(lane < points_s[c], 1.0, 0.0).astype(BF)
-            r = right_v[:, window] * mask
-            l = left_v[:, window] * mask
-            ext_v[c + HW] = r
-            masked_left_v[c] = l
-            rows += [r, l]
-        both = nt(jnp.concatenate(rows, axis=0), basis_v[g])
-        leaf = both[: 2 * rhs]
-        for u in range(1, pack):
-            leaf = jnp.where(lane2 < u * rank, leaf, both[2 * rhs * u : 2 * rhs * (u + 1)])
-        high, low = split(leaf)
-        leaf_v[: 2 * rhs, g * B : (g + 1) * B] = high
-        leaf_v[2 * rhs :, g * B : (g + 1) * B] = low
-
-    for g in range(clusters // pack):
-        leaf_step(g)
-    inputs[3].wait()
-    inputs[4].wait()
-    transfer2_v[...] = wide(transfer_v[...])
-    lift2_v[...] = wide(lift_v[...])
-    both = nn(leaf_v[...], transfer2_v[...])
-    k2 = transfer_v.shape[1]
-    parent = both[: 2 * rhs, :k2] + both[2 * rhs :, :k2] + both[: 2 * rhs, k2:]
-
-    def spot(slab, leaf):
-        return (leaf % CORES) * group + slab * chips + leaf // CORES
-
-    parents_v[spot(my_slab, my_leaf)] = parent[:rhs].astype(BF)
-    share = three_nn(parent, lift2_v[...])
-    for j in range(leaves):
-        share_v[j] = share[j * chunk : (j + 1) * chunk]
-
-    pl.semaphore_wait(barrier, leaves - 1 + slabs - 1 + after + before)
-
-    def remote(src, dst, send, recv, device):
-        return pltpu.make_async_remote_copy(
-            src_ref=src,
-            dst_ref=dst,
-            send_sem=send,
-            recv_sem=recv,
-            device_id=device,
-            device_id_type=MESH,
-        )
-
-    def share_copy(k):
-        peer = (my_leaf + k) % leaves
-        return remote(
-            share_v.at[peer],
-            share_in_v.at[my_leaf],
-            share_send.at[k],
-            share_recv.at[k],
-            (my_slab, peer),
-        )
-
-    def share_arrival(k):
-        peer = (my_leaf + leaves - k) % leaves
-        return remote(
-            share_v.at[my_leaf],
-            share_in_v.at[peer],
-            share_send.at[k],
-            share_recv.at[k],
-            (my_slab, peer),
-        )
-
-    def slab_copy(k):
-        return remote(
-            slab_v.at[my_slab],
-            slab_v.at[my_slab],
-            slab_send.at[k],
-            slab_recv.at[k],
-            ((my_slab + k) % slabs, my_leaf),
-        )
-
-    def slab_arrival(k):
-        peer = (my_slab + slabs - k) % slabs
-        return remote(
-            slab_v.at[my_slab],
-            slab_v.at[peer],
-            slab_send.at[k],
-            slab_recv.at[k],
-            (peer, my_leaf),
-        )
-
-    def top_copy(k):
-        return remote(
-            top_v.at[my_leaf],
-            top_v.at[my_leaf],
-            top_send.at[k],
-            top_recv.at[k],
-            (my_slab, (my_leaf + k) % leaves),
-        )
-
-    def top_arrival(k):
-        peer = (my_leaf + leaves - k) % leaves
-        return remote(
-            top_v.at[my_leaf],
-            top_v.at[peer],
-            top_send.at[k],
-            top_recv.at[k],
-            (my_slab, peer),
-        )
-
-    def chip_leaf(k):
-        return ((my_chip + k) % chips) * CORES + my_core
-
-    def parent_chip_copy(k):
-        at = spot(my_slab, my_leaf)
-        return remote(
-            parents_v.at[at],
-            parents_v.at[at],
-            pchip_send.at[k],
-            pchip_recv.at[k],
-            (my_slab, chip_leaf(k)),
-        )
-
-    def parent_chip_arrival(k):
-        leaf = chip_leaf(chips - k)
-        return remote(
-            parents_v.at[spot(my_slab, my_leaf)],
-            parents_v.at[spot(my_slab, leaf)],
-            pchip_send.at[k],
-            pchip_recv.at[k],
-            (my_slab, leaf),
-        )
-
-    def column(core, slab):
-        return parents_v.at[pl.ds(core * group + slab * chips, chips)]
-
-    def parent_slab_copy(k):
-        return remote(
-            column(my_core, my_slab),
-            column(my_core, my_slab),
-            pslab_send.at[k],
-            pslab_recv.at[k],
-            ((my_slab + k) % slabs, my_leaf),
-        )
-
-    def parent_slab_arrival(k):
-        peer = (my_slab + slabs - k) % slabs
-        return remote(
-            column(my_core, my_slab),
-            column(my_core, peer),
-            pslab_send.at[k],
-            pslab_recv.at[k],
-            (peer, my_leaf),
-        )
-
-    partner = (my_slab, my_chip * CORES + 1 - my_core)
-
-    def parent_core_copy():
-        half = parents_v.at[pl.ds(my_core * group, group)]
-        return remote(half, half, core_send.at[0], core_recv.at[0], partner)
-
-    def parent_core_arrival():
-        half = parents_v.at[pl.ds(my_core * group, group)]
-        other = parents_v.at[pl.ds((1 - my_core) * group, group)]
-        return remote(half, other, core_send.at[0], core_recv.at[0], partner)
-
-    def outward_core_copy():
-        return remote(core_out_v, core_in_v, core_send.at[1], core_recv.at[1], partner)
-
-    def outward_slab_copy(k):
-        peer = (my_slab + k) % slabs
-        return remote(
-            slab_out_v.at[peer],
-            slab_in_v.at[my_slab],
-            oslab_send.at[k],
-            oslab_recv.at[k],
-            (peer, my_leaf),
-        )
-
-    def outward_slab_arrival(k):
-        peer = (my_slab + slabs - k) % slabs
-        return remote(
-            slab_out_v.at[my_slab],
-            slab_in_v.at[peer],
-            oslab_send.at[k],
-            oslab_recv.at[k],
-            (peer, my_leaf),
-        )
-
-    def outward_chip_copy(k):
-        peer = (my_chip + k) % chips
-        return remote(
-            chip_out_v.at[peer],
-            chip_in_v.at[my_chip],
-            ochip_send.at[k],
-            ochip_recv.at[k],
-            (my_slab, chip_leaf(k)),
-        )
-
-    def outward_chip_arrival(k):
-        peer = (my_chip + chips - k) % chips
-        return remote(
-            chip_out_v.at[my_chip],
-            chip_in_v.at[peer],
-            ochip_send.at[k],
-            ochip_recv.at[k],
-            (my_slab, chip_leaf(chips - k)),
-        )
-
-    def halo_copy(to_next):
-        where = me + 1 if to_next else me - 1
-        src = clusters if to_next else HW
-        dst = 0 if to_next else clusters + HW
-        i = 0 if to_next else 1
-        return remote(
-            ext_v.at[pl.ds(src, HW)],
-            ext_v.at[pl.ds(dst, HW)],
-            halo_send.at[i],
-            halo_recv.at[i],
-            place(where),
-        )
-
-    def edge_copy(to_next):
-        i = 1 if to_next else 0
-        return remote(
-            edge_out_v.at[i],
-            edge_in_v.at[i],
-            edge_send.at[i],
-            edge_recv.at[i],
-            place(me + 1 if to_next else me - 1),
-        )
-
-    loop(1, leaves, lambda k: share_copy(k).start())
-    loop(1, chips, lambda k: parent_chip_copy(k).start())
-    share_in_v[my_leaf] = share_v[my_leaf]
-
-    @pl.when(me < devices - 1)
-    def _():
-        halo_copy(True).start()
-
-    @pl.when(me > 0)
-    def _():
-        halo_copy(False).start()
-
     inputs[5].wait()
     left_both = stacked(parent[rhs:])
 
@@ -535,33 +527,6 @@
     apex_row.wait()
     for t in range(slabs):
         apex2_v[t] = wide(apex_v[t])
-
-    inputs[6].wait()
-
-    def near_back(i, e0):
-        left = masked_left_v[i]
-        for w in range(width):
-            collected_v[e0 + w] += nn(left, near_v[table_s[w, i]])
-
-    def near_forward(i):
-        blocks = jnp.concatenate([near_v[i * slots + s] for s in range(slots)], axis=1)
-        picked = jnp.concatenate([ext_v[table_s[width + s, i]] for s in range(slots)], axis=1)
-        near_out_v[i] = nt(picked, blocks)
-
-    for i in range(HW):
-        near_back(i, i + first * (HW - i))
-    for i in range(clusters - HW, clusters):
-        near_back(i, i - last * (i - (clusters - HW - 1)))
-
-    edge_out_v[0] = collected_v[0:HW].astype(BF)
-    edge_out_v[1] = collected_v[clusters + HW :].astype(BF)
-
-    loop(1, leaves, lambda k: share_arrival(k).wait_recv())
-    total = share_in_v[0]
-    for j in range(1, leaves):
-        total = total + share_in_v[j]
-    slab_v[my_slab] = total
-    loop(1, slabs, lambda k: slab_copy(k).start())
 
     outward_core_copy().wait_recv()
     for slab in range(slabs):
@@ -572,8 +537,43 @@
     for chip in range(chips):
         own_v[chip] = owned(my_slab, chip, my_core) + core_in_v[my_slab * chips + chip]
 
+    loop(1, leaves, lambda k: share_arrival(k).wait_recv())
+    total = share_in_v[0]
+    for j in range(1, leaves):
+        total = total + share_in_v[j]
+    slab_v[my_slab] = total
+    loop(1, slabs, lambda k: slab_copy(k).start())
+
     loop(1, chips, lambda k: parent_chip_arrival(k).wait_recv())
     loop(1, slabs, lambda k: parent_slab_copy(k).start())
+
+    @pl.when(me < devices - 1)
+    def _():
+        halo_copy(True).start()
+
+    @pl.when(me > 0)
+    def _():
+        halo_copy(False).start()
+
+    inputs[6].wait()
+
+    def near_back(i, e0):
+        left = masked_left_v[i]
+        for w in range(width):
+            collected_v[e0 + w] += nn(left, near_v[table_s[w, i]])
+
+    def near_forward(i):
+        blocks = jnp.concatenate([near_v[i * slots + s] for s in range(slots)], axis=1)
+        picked = jnp.concatenate([ext_v[table_s[width + s, i]] for s in range(slots)], axis=1)
+        near_out_v[i] = nt(picked, blocks)
+
+    for i in range(HW):
+        near_back(i, i + first * (HW - i))
+    for i in range(clusters - HW, clusters):
+        near_back(i, i - last * (i - (clusters - HW - 1)))
+
+    edge_out_v[0] = collected_v[0:HW].astype(BF)
+    edge_out_v[1] = collected_v[clusters + HW :].astype(BF)
 
     @pl.when(me < devices - 1)
     def _():
@@ -593,7 +593,7 @@
             collected_v[i + e] += nn(left, blocks)
 
     middles = (clusters - 2 * HW) // HW
-    loop(0, middles // 2, middle_back)
+    loop(0, middles, middle_back)
 
     loop(1, slabs, lambda k: slab_arrival(k).wait_recv())
 
@@ -625,8 +625,6 @@
 
     loop(1, slabs, lambda k: parent_slab_arrival(k).wait_recv())
     parent_core_copy().start()
-
-    loop(middles // 2, middles, middle_back)
 
     @pl.when(me > 0)
     def _():
@@ -678,30 +676,7 @@
     loop(1, leaves, lambda k: top_arrival(k).wait_recv())
     top = jnp.concatenate([top_v[j] for j in range(leaves)], axis=0)
     hat = three_nt(top, lift2_v[...]) + jnp.concatenate([far_right, far_left], axis=0)
-    hat2 = paired_rows(hat)
-    span = 2 * B
-    for n in range(clusters * rank // span):
-        both = nt(hat2, transfer2_v[n * span : (n + 1) * span])
-        down = (both[: 2 * rhs] + both[2 * rhs :]).astype(BF)
-        for h in range(span // B):
-            g = n * (span // B) + h
-            piece = down[:, h * B : (h + 1) * B]
-            rows = [
-                jnp.where((lane2 >= u * rank) & (lane2 < (u + 1) * rank), piece, jnp.zeros_like(piece))
-                for u in range(pack)
-            ]
-            out = nn(jnp.concatenate(rows, axis=0), basis_v[g])
-            for u in range(pack):
-                c = g * pack + u
-                keep = lane < points_s[c]
-                base = 2 * rhs * u
-                window = slice(c * B, (c + 1) * B)
-                product_ref[:, window] = jnp.where(
-                    keep, near_out_v[c] + out[base : base + rhs], 0.0
-                )
-                adjoint_ref[:, window] = jnp.where(
-                    keep, collected_v[c + HW] + out[base + rhs : base + 2 * rhs], 0.0
-                )
+    hat_ref[...] = paired_rows(hat)
 
     loop(1, leaves, lambda k: share_copy(k).wait_send())
     loop(1, leaves, lambda k: top_copy(k).wait_send())
@@ -722,6 +697,56 @@
     def _():
         halo_copy(False).wait_send()
         edge_copy(False).wait_send()
+
+
+def finish_kernel(
+    pack,
+    hat_ref,
+    near_ref,
+    back_ref,
+    transfer_ref,
+    basis_ref,
+    keep_ref,
+    product_h,
+    adjoint_h,
+    product_v,
+    adjoint_v,
+    sem,
+):
+    rhs = product_v.shape[0]
+    rank = B // pack
+    span = 2 * B
+    pieces = transfer_ref.shape[0] // span
+    lane2 = lax.broadcasted_iota(jnp.int32, (2 * rhs, B), 1)
+    hat2 = hat_ref[...]
+    copies = []
+    for n in range(pieces):
+        both = nt(hat2, transfer_ref[n * span : (n + 1) * span])
+        down = (both[: 2 * rhs] + both[2 * rhs :]).astype(BF)
+        for h in range(span // B):
+            g = n * (span // B) + h
+            piece = down[:, h * B : (h + 1) * B]
+            rows = [
+                jnp.where((lane2 >= u * rank) & (lane2 < (u + 1) * rank), piece, jnp.zeros_like(piece))
+                for u in range(pack)
+            ]
+            out = nn(jnp.concatenate(rows, axis=0), basis_ref[g])
+            for u in range(pack):
+                c = g * pack + u
+                keep = keep_ref[c : c + 1] > 0.0
+                base = 2 * rhs * u
+                window = slice(c * B, (c + 1) * B)
+                product_v[:, window] = jnp.where(keep, near_ref[c] + out[base : base + rhs], 0.0)
+                adjoint_v[:, window] = jnp.where(
+                    keep, back_ref[c + HW] + out[base + rhs : base + 2 * rhs], 0.0
+                )
+        part = pl.ds(n * pack * span, pack * span)
+        for i, (src, dst) in enumerate([(product_v, product_h), (adjoint_v, adjoint_h)]):
+            copy = pltpu.make_async_copy(src.at[:, part], dst.at[:, part], sem.at[i, n])
+            copy.start()
+            copies.append(copy)
+    for copy in copies:
+        copy.wait()
 
 
 def shards(
@@ -754,15 +779,21 @@
     vmem = pl.BlockSpec(memory_space=pltpu.VMEM)
     dma = pltpu.SemaphoreType.DMA
     out = jax.ShapeDtypeStruct((rhs, columns), F32)
-    return pl.pallas_call(
+    held = pl.pallas_call(
         functools.partial(kernel, slabs, leaves),
-        out_shape=(out, out),
+        out_shape=(
+            jax.ShapeDtypeStruct((4 * rhs, 2 * k2), BF),
+            jax.ShapeDtypeStruct((clusters, rhs, B), F32),
+            jax.ShapeDtypeStruct((clusters + 2 * HW, rhs, B), F32),
+            jax.ShapeDtypeStruct((clusters * rank, 2 * k2), BF),
+            jax.ShapeDtypeStruct((clusters // pack, B, B), BF),
+            jax.ShapeDtypeStruct((clusters, B), F32),
+        ),
         in_specs=[pl.BlockSpec(memory_space=pltpu.SMEM)] + [hbm] * 11,
-        out_specs=(vmem, vmem),
+        out_specs=(vmem,) * 6,
         scratch_shapes=[
             pltpu.VMEM((rhs, columns), BF),
             pltpu.VMEM((rhs, columns), BF),
-            pltpu.VMEM((clusters // pack, B, B), BF),
             pltpu.VMEM((clusters * rank, k2), F32),
             pltpu.VMEM((k2, k3), F32),
             pltpu.VMEM(coupling.shape[1:], F32),
@@ -778,12 +809,9 @@
             pltpu.VMEM((clusters + 2 * HW, rhs, B), BF),
             pltpu.VMEM((clusters, rhs, B), BF),
             pltpu.VMEM((4 * rhs, clusters * rank), BF),
-            pltpu.VMEM((clusters * rank, 2 * k2), BF),
             pltpu.VMEM((k2, 2 * k3), BF),
             pltpu.VMEM((far_slots, k2, 2 * k2), BF),
             pltpu.VMEM((slabs, k3, 2 * k3), BF),
-            pltpu.VMEM((clusters + 2 * HW, rhs, B), F32),
-            pltpu.VMEM((clusters, rhs, B), F32),
             pltpu.VMEM((2, HW, rhs, B), BF),
             pltpu.VMEM((2, HW, rhs, B), BF),
             pltpu.VMEM((leaves, chunk, k3), F32),
@@ -845,6 +873,20 @@
             )
         ],
     )
+    pieces = clusters * rank // (2 * B)
+    return pl.pallas_call(
+        functools.partial(finish_kernel, pack),
+        out_shape=(out, out),
+        in_specs=[vmem] * 6,
+        out_specs=(hbm, hbm),
+        scratch_shapes=[
+            pltpu.VMEM((rhs, columns), F32),
+            pltpu.VMEM((rhs, columns), F32),
+            dma((2, pieces)),
+        ],
+        compiler_params=pltpu.CompilerParams(vmem_limit_bytes=8 * 1024 * 1024),
+        name="h2_finish",
+    )(*held)
 
 
 def solution(mesh):

time: 26.4 us -> 23.9 us (0.905)
  local copies, waits for them, and re-layouts: 1.59 us -> 0 us
  Pallas kernels: 23.4 us -> 22.5 us
    unnamed x2 -> x0, local copies, waits for them, and re-layouts: 1.59 us -> none
    pallas_call x1 -> x2, Pallas kernels: 23.4 us -> 22.5 us  [the longest x1 20.2 us: shards(): pl.pallas_call(functools.partial(kernel, slabs, leaves), out_shape=(jax.S...]
where the time goes in v2:
time: 23.9 us; the launch traced here: 23.8 us
  Pallas kernels  22.5 us (94%)
  between operations  1.29 us (5%)
    pallas_call x1, Pallas kernels, shards(): pl.pallas_call(functools.partial(kernel, slabs, leaves), out_shape=(jax.S...  20.2 us
    pallas_call x1, Pallas kernels, shards(): pl.pallas_call(functools.partial(finish_kernel, pack), out_shape=(out, ou...  2.27 us

profile of v2, /device:TPU:0, one launch (start us, length us, event | category | flops | bytes accessed | tf_op | source)
XLA Modules:
  0.0 23.8 jit_solution(8551204639935346129)
XLA Ops:
  1.3 20.2 %h2_step.1 = (bf16[128,256]{1,0:T(8,128)(2,1)S(1)}, f32[32,32,128]{2,1,0:T(8,128)S(1)}, f32[40,32,128]{2,1,0:T(8,128)S(1)}, bf16[2048,256]{1,0:T(8,128)(2,1)S(1)...) custom-call(s32[1]{0:T(128)S(6)} %copy.14.count_s, s32[32]{0:T(128)} %points_h.1, s32[24]{0:T(128)} %bitcast.13, ...), custom_call_target="tpu_custom_call" | custom-call | tf_op jit(solution)/shard_map/h2_step/pallas_call | solution.py:782
  21.5 2.3 %h2_finish.1 = (f32[32,4096]{1,0:T(8,128)}, f32[32,4096]{1,0:T(8,128)}) custom-call(bf16[128,256]{1,0:T(8,128)(2,1)S(1)} %get-tuple-element.8.hat_ref, f32[32,32,128]{2,1,0:T(8,128)S(1)} %get-tuple-element.9.near_ref, f32[40,32,128]{2,1,0:T(8,128)S(1)} %get-tuple-element.10.back_ref, bf16[2048,256]{1,0:T(8,128)(2,1)S(1)} %get-tuple-element.11.transfer_ref, ...), custom_call_target="tpu_custom_call" | custom-call | tf_op jit(solution)/shard_map/h2_finish/pallas_call | solution.py:877
